TPU v7x, 256 devices: a whole 4x4x8 slice. The times are simulated.
256 devices in a mesh: ctx: 64 (over z, x, core), heads: 4 (over y).
Axes of the slice: x: 4, y: 4, z: 8, core: 2. Of those that a mesh axis runs over, the one named last changes fastest.
Arguments:
- q_raw: bfloat16 [16384, 8192], P('ctx', 'heads'), may hold values from -60 to 60
- k_raw: bfloat16 [16384, 1024], P('ctx', 'heads'), may hold values from -60 to 60
- values: bfloat16 [16384, 1024], P('ctx', 'heads'), may hold values from -6 to 6
- saved_out: bfloat16 [16384, 8192], P('ctx', 'heads'), may hold values from -6 to 6
- out_grad: bfloat16 [16384, 8192], P('ctx', 'heads'), may hold values from -60 to 60
- q_gain: float32 [128], replicated, may hold values from 0.25 to 1.75
- k_gain: float32 [128], replicated, may hold values from 0.25 to 1.75
- ancestors: int32 [256, 32], P('ctx'), may hold values from -1 to 255, as said below
Outputs:
- dq_raw: bfloat16 [16384, 8192], P('ctx', 'heads')
- dk_raw: bfloat16 [16384, 1024], P('ctx', 'heads')
- dv: bfloat16 [16384, 1024], P('ctx', 'heads')
- q_gain_grad: float32 [128], replicated
- k_gain_grad: float32 [128], replicated
Inputs may be any that keep to these rules, and one draw needn't show every extreme that they name: `ancestors`: the forest is 8 trees of 32 blocks each; in tree order, tree k holds blocks (k * 32 + 256 / 64 + b) mod 256 for b = 0 to 31. Row b lists, in tree order, every block on the path from its tree's first block to b, ending with b itself, then -1s. The first 16 blocks of a tree form its prompt, each the child of the block before it; every other block's parent is a block earlier in its tree, from the prompt's last block on.
All inputs are finite; a program needn't handle non-finite values.
Results may differ from a plain program's by a relative error of at most 0.0069.
Values may be sent and summed in bfloat16 or wider, within the bound.
A program may use at most 64 MiB of HBM per device.

v0:
```python
import math
import jax
import jax.numpy as jnp
from jax import lax
from jax.sharding import PartitionSpec as P

TREE_DEV = 8
ROPE_BASE = 1000000.0
EPS = 1e-06


def passed_along(value, axis, steps):
    count = lax.axis_size(axis)
    pairs = [(source, (source + steps) % count) for source in range(count)]
    return lax.ppermute(value, axis, pairs)


def rope_tables(positions, head_dim):
    half_dim = head_dim // 2
    frequency = jnp.exp(
        jnp.arange(half_dim, dtype=jnp.float32) * (-2.0 * math.log(ROPE_BASE) / head_dim)
    )
    angles = positions.astype(jnp.float32)[:, None] * frequency[None, :]
    return (jnp.cos(angles), jnp.sin(angles))


def norm_rope(inputs, gain_vec, cos_table, sin_table):
    recip_rms = lax.rsqrt(jnp.mean(inputs * inputs, -1, keepdims=True) + EPS)
    scaled = inputs * recip_rms * gain_vec
    half_dim = inputs.shape[-1] // 2
    cos_part = cos_table[:, None, :]
    sin_part = sin_table[:, None, :]
    front_half = scaled[..., :half_dim]
    back_half = scaled[..., half_dim:]
    return jnp.concatenate(
        [
            front_half * cos_part - back_half * sin_part,
            back_half * cos_part + front_half * sin_part,
        ],
        -1,
    )


def norm_rope_back(inputs, gain_vec, cos_table, sin_table, upstream):
    half_dim = inputs.shape[-1] // 2
    cos_part = cos_table[:, None, :]
    sin_part = sin_table[:, None, :]
    front_half = upstream[..., :half_dim]
    back_half = upstream[..., half_dim:]
    unrotated = jnp.concatenate(
        [
            front_half * cos_part + back_half * sin_part,
            back_half * cos_part - front_half * sin_part,
        ],
        -1,
    )
    recip_rms = lax.rsqrt(jnp.mean(inputs * inputs, -1, keepdims=True) + EPS)
    normed = inputs * recip_rms
    gain_term = jnp.sum(unrotated * normed, axis=(0, 1))
    gain_grad = unrotated * gain_vec
    input_grad = recip_rms * (gain_grad - normed * jnp.mean(gain_grad * normed, -1, keepdims=True))
    return (input_grad, gain_term)


def on_device(q_raw, k_raw, values, saved_out, out_grad, q_gain, k_gain, ancestors):
    tokens_here = q_raw.shape[0]
    head_dim = q_gain.shape[0]
    kv_local = k_raw.shape[1] // head_dim
    group_size = q_raw.shape[1] // (kv_local * head_dim)
    block_count = ancestors.shape[0]
    block_len = tokens_here // block_count
    cycle_size = lax.axis_size("ctx")
    my_index = lax.axis_index("ctx")
    hop_count = TREE_DEV - 1
    inv_root = 1.0 / math.sqrt(head_dim)
    offsets = jnp.arange(block_len, dtype=jnp.int32)
    depth_count = jnp.sum((ancestors >= 0).astype(jnp.int32), 1)
    positions = (((depth_count - 1) * block_len)[:, None] + offsets[None, :]).reshape(tokens_here)
    cos_table, sin_table = rope_tables(positions, head_dim)
    q_float = q_raw.astype(jnp.float32).reshape(tokens_here, kv_local * group_size, head_dim)
    k_float = k_raw.astype(jnp.float32).reshape(tokens_here, kv_local, head_dim)
    q_rot = norm_rope(q_float, q_gain, cos_table, sin_table).astype(jnp.bfloat16)
    q_rot = q_rot.reshape(tokens_here, kv_local, group_size, head_dim)
    k_rot = norm_rope(k_float, k_gain, cos_table, sin_table).astype(jnp.bfloat16)
    v_heads = values.reshape(tokens_here, kv_local, head_dim)
    grad_heads = out_grad.reshape(tokens_here, kv_local, group_size, head_dim)
    out_heads = saved_out.reshape(tokens_here, kv_local, group_size, head_dim)
    row_delta = jnp.einsum(
        "ikgd,ikgd->kgi", grad_heads, out_heads, preferred_element_type=jnp.float32
    )
    key_value = jnp.stack((k_rot, v_heads), 1)
    local_tok = jnp.arange(tokens_here, dtype=jnp.int32)

    def visible(source):
        key_blocks = source * block_count + jnp.arange(block_count, dtype=jnp.int32)
        block_vis = jnp.any(ancestors[:, :, None] == key_blocks[None, None, :], axis=1)
        token_vis = jnp.repeat(jnp.repeat(block_vis, block_len, 0), block_len, 1)
        causal = (local_tok[None, :] <= local_tok[:, None]) | (source != my_index)
        return (token_vis & causal, jnp.any(block_vis))

    def scores_of(key_rot):
        return (
            jnp.einsum("ikgd,jkd->kgij", q_rot, key_rot, preferred_element_type=jnp.float32)
            * inv_root
        )

    def add_mass(exp_mass, key_rot, allowed):
        expo = jnp.where(allowed[None, None], jnp.exp(scores_of(key_rot)), 0.0)
        return exp_mass + jnp.sum(expo, -1)

    def accumulate(exp_mass, key_rot, allowed):
        return add_mass(exp_mass, key_rot, allowed)

    own_allowed, own_touched = visible(my_index)
    exp_mass = add_mass(
        jnp.zeros((kv_local, group_size, tokens_here), jnp.float32), k_rot, own_allowed
    )

    def forward_step(hop_index, loop_state):
        mass_now, moving = loop_state
        moving = passed_along(moving, "ctx", 1)
        allowed, touched = visible((my_index - hop_index) % cycle_size)
        return (accumulate(mass_now, moving, allowed), moving)

    exp_mass, _ = lax.fori_loop(1, hop_count + 1, forward_step, (exp_mass, k_rot))
    log_mass = jnp.log(exp_mass)

    def grad_terms(key_rot, val_rot, allowed):
        weights = jnp.where(
            allowed[None, None], jnp.exp(scores_of(key_rot) - log_mass[..., None]), 0.0
        )
        weights_low = weights.astype(jnp.bfloat16)
        grad_prob = jnp.einsum(
            "ikgd,jkd->kgij", grad_heads, val_rot, preferred_element_type=jnp.float32
        )
        dscore = (weights * (grad_prob - row_delta[..., None]) * inv_root).astype(jnp.bfloat16)
        dq_part = jnp.einsum("kgij,jkd->ikgd", dscore, key_rot, preferred_element_type=jnp.float32)
        dk_part = jnp.einsum("kgij,ikgd->jkd", dscore, q_rot, preferred_element_type=jnp.float32)
        dv_part = jnp.einsum(
            "kgij,ikgd->jkd", weights_low, grad_heads, preferred_element_type=jnp.float32
        )
        return (dq_part, jnp.stack((dk_part, dv_part), 1))

    def pair_terms(moving, allowed):
        return grad_terms(moving[:, 0], moving[:, 1], allowed)

    dq_acc, own_part = grad_terms(k_rot, v_heads, own_allowed)
    key_grads = own_part

    def back_step(hop_index, loop_state):
        dq_now, grads_now, moving = loop_state
        moving = passed_along(moving, "ctx", 1)
        source = (my_index - hop_index) % cycle_size
        allowed, touched = visible(source)
        dq_part, kv_part = pair_terms(moving, allowed)
        grads_now = passed_along(grads_now, "ctx", 1) + kv_part
        return (dq_now + dq_part, grads_now, moving)

    dq_acc, key_grads, _ = lax.fori_loop(
        1, hop_count + 1, back_step, (dq_acc, key_grads, key_value)
    )
    key_grads = passed_along(key_grads, "ctx", -hop_count)
    dq_rot = dq_acc.reshape(tokens_here, kv_local * group_size, head_dim)
    dq_input, q_gain_part = norm_rope_back(q_float, q_gain, cos_table, sin_table, dq_rot)
    dk_input, k_gain_part = norm_rope_back(k_float, k_gain, cos_table, sin_table, key_grads[:, 0])
    q_gain_grad, k_gain_grad = lax.psum((q_gain_part, k_gain_part), ("ctx", "heads"))
    dq_raw = dq_input.astype(jnp.bfloat16).reshape(tokens_here, kv_local * group_size * head_dim)
    dk_raw = dk_input.astype(jnp.bfloat16).reshape(tokens_here, kv_local * head_dim)
    dv = key_grads[:, 1].astype(jnp.bfloat16).reshape(tokens_here, kv_local * head_dim)
    return (dq_raw, dk_raw, dv, q_gain_grad, k_gain_grad)


def solution(mesh):
    in_specs = (
        P("ctx", "heads"),
        P("ctx", "heads"),
        P("ctx", "heads"),
        P("ctx", "heads"),
        P("ctx", "heads"),
        P(),
        P(),
        P("ctx", None),
    )
    out_specs = (P("ctx", "heads"), P("ctx", "heads"), P("ctx", "heads"), P(), P())
    return jax.shard_map(
        on_device, mesh=mesh, in_specs=in_specs, out_specs=out_specs, check_vma=False
    )
```

profile of v0, /device:TPU:1, one launch (start us, length us, event | category | flops | bytes accessed | tf_op | source)
XLA Modules:
  0.0 316.6 jit_solution(3900875006757037314)
XLA Ops:
  11.5 2.9 fusion.29
  14.4 59.1 %while.38 = (s32[]{:T(128)}, f32[2,8,256]{2,1,0:T(8,128)S(1)}, bf16[256,2,128]{2,0,1:T(8,128)(2,1)S(1)}, s32[4,32]{1,0:T(4,128)S(1)}, s32[]{:T(128)}, /*index=5*...) while((s32[]{:T(128)}, f32[2,8,256]{2,1,0:T(8,128)S(1)}, ...), condition=%wide.region_8.9_spmd.clone, body=%wide.region_5.8_spmd.clone.sunk | while | flops 271778816 | bytes 2167688 | solution.py:125
  14.4 2.6 collective-permute-start
  20.0 2.5 collective-permute-start
  23.1 4.9 %collective-permute-done = bf16[256,2,128]{2,0,1:T(8,128)(2,1)S(1)} collective-permute-done((bf16[256,2,128]{2,0,1:T(8,128)(2,1)S(1)}, bf16[256,2,128]{2,0,1:T(8,128)(2,1)S(1)}, u32[]{:S(2)}, u32[]{:S(2)}) %collective-permute-start) | collective-permute-done | bytes 131104 | tf_op jit(solution)/shard_map/while/body/eval_jaxpr/ppermute | solution.py:15
  29.8 7.1 %collective-permute-done = bf16[256,2,128]{2,0,1:T(8,128)(2,1)S(1)} collective-permute-done((bf16[256,2,128]{2,0,1:T(8,128)(2,1)S(1)}, bf16[256,2,128]{2,0,1:T(8,128)(2,1)S(1)}, u32[]{:S(2)}, u32[]{:S(2)}) %collective-permute-start) | collective-permute-done | bytes 131104 | tf_op jit(solution)/shard_map/while/body/eval_jaxpr/ppermute | solution.py:15
  38.7 7.1 %collective-permute-done = bf16[256,2,128]{2,0,1:T(8,128)(2,1)S(1)} collective-permute-done((bf16[256,2,128]{2,0,1:T(8,128)(2,1)S(1)}, bf16[256,2,128]{2,0,1:T(8,128)(2,1)S(1)}, u32[]{:S(2)}, u32[]{:S(2)}) %collective-permute-start) | collective-permute-done | bytes 131104 | tf_op jit(solution)/shard_map/while/body/eval_jaxpr/ppermute | solution.py:15
  47.5 7.1 %collective-permute-done = bf16[256,2,128]{2,0,1:T(8,128)(2,1)S(1)} collective-permute-done((bf16[256,2,128]{2,0,1:T(8,128)(2,1)S(1)}, bf16[256,2,128]{2,0,1:T(8,128)(2,1)S(1)}, u32[]{:S(2)}, u32[]{:S(2)}) %collective-permute-start) | collective-permute-done | bytes 131104 | tf_op jit(solution)/shard_map/while/body/eval_jaxpr/ppermute | solution.py:15
  56.4 7.1 %collective-permute-done = bf16[256,2,128]{2,0,1:T(8,128)(2,1)S(1)} collective-permute-done((bf16[256,2,128]{2,0,1:T(8,128)(2,1)S(1)}, bf16[256,2,128]{2,0,1:T(8,128)(2,1)S(1)}, u32[]{:S(2)}, u32[]{:S(2)}) %collective-permute-start) | collective-permute-done | bytes 131104 | tf_op jit(solution)/shard_map/while/body/eval_jaxpr/ppermute | solution.py:15
  65.3 7.1 %collective-permute-done = bf16[256,2,128]{2,0,1:T(8,128)(2,1)S(1)} collective-permute-done((bf16[256,2,128]{2,0,1:T(8,128)(2,1)S(1)}, bf16[256,2,128]{2,0,1:T(8,128)(2,1)S(1)}, u32[]{:S(2)}, u32[]{:S(2)}) %collective-permute-start) | collective-permute-done | bytes 131104 | tf_op jit(solution)/shard_map/while/body/eval_jaxpr/ppermute | solution.py:15
  79.2 3.3 %fusion.40 = f32[256,1,2,128]{0,3,2,1:T(8,128)S(1)} fusion(bf16[256,2,8,128]{0,3,2,1:T(8,128)(2,1)S(1)} %bitcast.262, f32[2,256,256,8]{2,1,3,0:T(8,128)} %get-tuple-element.597, f32[2,8,256]{2,1,0:T(8,128)S(1)} %copy-done.24, pred[256,256]{0,1:T(8,128)(4,1)S(1)} %copy-done.21), kind=kOutput, calls=%fused_computation.66 | convolution fusion | flops 272629760 | bytes 5586944 | tf_op jit(solution)/shard_map/kgij,ikgd->jkd/dot_general | solution.py:139
  89.9 1.9 copy.98
  95.2 123.4 %while.39 = (s32[]{:T(128)}, f32[256,2,8,128]{3,0,2,1:T(8,128)S(1)}, f32[256,2,2,128]{3,0,2,1:T(8,128)}, bf16[256,2,2,128]{3,0,2,1:T(8,128)(2,1)}, s32[4,32]{1,0...) while((s32[]{:T(128)}, ...), condition=%wide.region_11.12_spmd.clone, body=%wide.region_9.11_spmd.clone.sunk | while | flops 1354695680 | bytes 37999652 | solution.py:159
  96.9 6.4 %collective-permute-done.1 = bf16[256,2,2,128]{3,0,2,1:T(8,128)(2,1)S(1)} collective-permute-done((bf16[256,2,2,128]{3,0,2,1:T(8,128)(2,1)}, bf16[256,2,2,128]{3,0,2,1:T(8,128)(2,1)S(1)}, u32[]{:S(2)}, u32[]{:S(2)}) %collective-permute-start.1) | collective-permute-done | bytes 262176 | tf_op jit(solution)/shard_map/while/body/eval_jaxpr/ppermute | solution.py:15
  113.5 7.6 %collective-permute-done.1 = bf16[256,2,2,128]{3,0,2,1:T(8,128)(2,1)S(1)} collective-permute-done((bf16[256,2,2,128]{3,0,2,1:T(8,128)(2,1)}, bf16[256,2,2,128]{3,0,2,1:T(8,128)(2,1)S(1)}, u32[]{:S(2)}, u32[]{:S(2)}) %collective-permute-start.1) | collective-permute-done | bytes 262176 | tf_op jit(solution)/shard_map/while/body/eval_jaxpr/ppermute | solution.py:15
  131.3 7.6 %collective-permute-done.1 = bf16[256,2,2,128]{3,0,2,1:T(8,128)(2,1)S(1)} collective-permute-done((bf16[256,2,2,128]{3,0,2,1:T(8,128)(2,1)}, bf16[256,2,2,128]{3,0,2,1:T(8,128)(2,1)S(1)}, u32[]{:S(2)}, u32[]{:S(2)}) %collective-permute-start.1) | collective-permute-done | bytes 262176 | tf_op jit(solution)/shard_map/while/body/eval_jaxpr/ppermute | solution.py:15
  149.1 7.6 %collective-permute-done.1 = bf16[256,2,2,128]{3,0,2,1:T(8,128)(2,1)S(1)} collective-permute-done((bf16[256,2,2,128]{3,0,2,1:T(8,128)(2,1)}, bf16[256,2,2,128]{3,0,2,1:T(8,128)(2,1)S(1)}, u32[]{:S(2)}, u32[]{:S(2)}) %collective-permute-start.1) | collective-permute-done | bytes 262176 | tf_op jit(solution)/shard_map/while/body/eval_jaxpr/ppermute | solution.py:15
  166.9 7.6 %collective-permute-done.1 = bf16[256,2,2,128]{3,0,2,1:T(8,128)(2,1)S(1)} collective-permute-done((bf16[256,2,2,128]{3,0,2,1:T(8,128)(2,1)}, bf16[256,2,2,128]{3,0,2,1:T(8,128)(2,1)S(1)}, u32[]{:S(2)}, u32[]{:S(2)}) %collective-permute-start.1) | collective-permute-done | bytes 262176 | tf_op jit(solution)/shard_map/while/body/eval_jaxpr/ppermute | solution.py:15
  184.7 7.6 %collective-permute-done.1 = bf16[256,2,2,128]{3,0,2,1:T(8,128)(2,1)S(1)} collective-permute-done((bf16[256,2,2,128]{3,0,2,1:T(8,128)(2,1)}, bf16[256,2,2,128]{3,0,2,1:T(8,128)(2,1)S(1)}, u32[]{:S(2)}, u32[]{:S(2)}) %collective-permute-start.1) | collective-permute-done | bytes 262176 | tf_op jit(solution)/shard_map/while/body/eval_jaxpr/ppermute | solution.py:15
  202.5 7.6 %collective-permute-done.1 = bf16[256,2,2,128]{3,0,2,1:T(8,128)(2,1)S(1)} collective-permute-done((bf16[256,2,2,128]{3,0,2,1:T(8,128)(2,1)}, bf16[256,2,2,128]{3,0,2,1:T(8,128)(2,1)S(1)}, u32[]{:S(2)}, u32[]{:S(2)}) %collective-permute-start.1) | collective-permute-done | bytes 262176 | tf_op jit(solution)/shard_map/while/body/eval_jaxpr/ppermute | solution.py:15
  220.2 2.5 multiply_add_fusion
  222.7 2.1 multiply_reduce_fusion.1
  226.0 3.8 %fusion.36 = (f32[2048]{0:T(1024)S(1)}, bf16[256,2048]{1,0:T(8,128)(2,1)}) fusion(bf16[256,2048]{1,0:T(8,128)(2,1)S(1)} %copy-done.3, f32[32,8,16,128]{3,2,1,0:T(8,128)S(1)} %bitcast.265, f32[32,8,16,128]{3,2,1,0:T(8,128)S(1)} %bitcast.267, f32[32,8,16,128]{3,2,1,0:T(8,128)S(1)} %bitcast.266, f32[2048]{0:T(1024)S(1)} %broadcast_bitcast_fusion), kind=kLoop, calls=%fused_computation.53 | loop fusion | flops 4716544 | bytes 8404992 | tf_op jit(solution)/shard_map/reduce_sum | solution.py:59
  232.6 84.0 %all-reduce = (f32[128]{0:T(128)}, f32[128]{0:T(128)}) all-reduce(f32[128]{0:T(128)S(1)} %bitcast_reduce_fusion, f32[128]{0:T(128)S(1)} %bitcast_reduce_fusion.1), channel_id=1, replica_groups=mesh['ctx'=64,'heads'=4] {'ctx','heads'}, use_global_device_ids=true, to_apply=%region_16.17 | all-reduce | flops 256 | bytes 2048 | tf_op jit(solution)/shard_map/psum | solution.py:166
  (344 shorter events, 116.3 us)
Async XLA Ops:
  1.8 5.1 %copy-start.6 = (f32[256,2,128]{2,0,1:T(8,128)}, f32[256,2,128]{2,0,1:T(8,128)S(1)}, u32[]{:S(2)}) copy-start(f32[256,2,128]{2,0,1:T(8,128)S(1)} %copy.83) | copy-start | bytes 786436
  14.4 59.7 %copy-start.14 = (bf16[256,2048]{1,0:T(8,128)(2,1)S(1)}, bf16[256,2048]{1,0:T(8,128)(2,1)}, u32[]{:S(2)}) copy-start(bf16[256,2048]{1,0:T(8,128)(2,1)} %param.16) | copy-start | bytes 3145732
  14.4 4.5 %collective-permute-start = (bf16[256,2,128]{2,0,1:T(8,128)(2,1)S(1)}, bf16[256,2,128]{2,0,1:T(8,128)(2,1)S(1)}, u32[]{:S(2)}, u32[]{:S(2)}) collective-permute-start(bf16[256,2,128]{2,0,1:T(8,128)(2,1)S(1)} %get-tuple-element.709), channel_id=1, source_target_pairs={{0,4},{4,8},{8,12},{12,16},{16,20},{20,24},{24,28},{28,32},{32,36}... | collective-permute-start | bytes 393224 | tf_op jit(solution)/shard_map/while/body/eval_jaxpr/ppermute | solution.py:15
  20.0 8.0 %collective-permute-start = (bf16[256,2,128]{2,0,1:T(8,128)(2,1)S(1)}, bf16[256,2,128]{2,0,1:T(8,128)(2,1)S(1)}, u32[]{:S(2)}, u32[]{:S(2)}) collective-permute-start(bf16[256,2,128]{2,0,1:T(8,128)(2,1)S(1)} %get-tuple-element.709), channel_id=1, source_target_pairs={{0,4},{4,8},{8,12},{12,16},{16,20},{20,24},{24,28},{28,32},{32,36}... | collective-permute-start | bytes 393224 | tf_op jit(solution)/shard_map/while/body/eval_jaxpr/ppermute | solution.py:15
  29.1 7.8 %collective-permute-start = (bf16[256,2,128]{2,0,1:T(8,128)(2,1)S(1)}, bf16[256,2,128]{2,0,1:T(8,128)(2,1)S(1)}, u32[]{:S(2)}, u32[]{:S(2)}) collective-permute-start(bf16[256,2,128]{2,0,1:T(8,128)(2,1)S(1)} %get-tuple-element.709), channel_id=1, source_target_pairs={{0,4},{4,8},{8,12},{12,16},{16,20},{20,24},{24,28},{28,32},{32,36}... | collective-permute-start | bytes 393224 | tf_op jit(solution)/shard_map/while/body/eval_jaxpr/ppermute | solution.py:15
  38.0 7.8 %collective-permute-start = (bf16[256,2,128]{2,0,1:T(8,128)(2,1)S(1)}, bf16[256,2,128]{2,0,1:T(8,128)(2,1)S(1)}, u32[]{:S(2)}, u32[]{:S(2)}) collective-permute-start(bf16[256,2,128]{2,0,1:T(8,128)(2,1)S(1)} %get-tuple-element.709), channel_id=1, source_target_pairs={{0,4},{4,8},{8,12},{12,16},{16,20},{20,24},{24,28},{28,32},{32,36}... | collective-permute-start | bytes 393224 | tf_op jit(solution)/shard_map/while/body/eval_jaxpr/ppermute | solution.py:15
  46.9 7.8 %collective-permute-start = (bf16[256,2,128]{2,0,1:T(8,128)(2,1)S(1)}, bf16[256,2,128]{2,0,1:T(8,128)(2,1)S(1)}, u32[]{:S(2)}, u32[]{:S(2)}) collective-permute-start(bf16[256,2,128]{2,0,1:T(8,128)(2,1)S(1)} %get-tuple-element.709), channel_id=1, source_target_pairs={{0,4},{4,8},{8,12},{12,16},{16,20},{20,24},{24,28},{28,32},{32,36}... | collective-permute-start | bytes 393224 | tf_op jit(solution)/shard_map/while/body/eval_jaxpr/ppermute | solution.py:15
  55.7 7.8 %collective-permute-start = (bf16[256,2,128]{2,0,1:T(8,128)(2,1)S(1)}, bf16[256,2,128]{2,0,1:T(8,128)(2,1)S(1)}, u32[]{:S(2)}, u32[]{:S(2)}) collective-permute-start(bf16[256,2,128]{2,0,1:T(8,128)(2,1)S(1)} %get-tuple-element.709), channel_id=1, source_target_pairs={{0,4},{4,8},{8,12},{12,16},{16,20},{20,24},{24,28},{28,32},{32,36}... | collective-permute-start | bytes 393224 | tf_op jit(solution)/shard_map/while/body/eval_jaxpr/ppermute | solution.py:15
  64.6 7.8 %collective-permute-start = (bf16[256,2,128]{2,0,1:T(8,128)(2,1)S(1)}, bf16[256,2,128]{2,0,1:T(8,128)(2,1)S(1)}, u32[]{:S(2)}, u32[]{:S(2)}) collective-permute-start(bf16[256,2,128]{2,0,1:T(8,128)(2,1)S(1)} %get-tuple-element.709), channel_id=1, source_target_pairs={{0,4},{4,8},{8,12},{12,16},{16,20},{20,24},{24,28},{28,32},{32,36}... | collective-permute-start | bytes 393224 | tf_op jit(solution)/shard_map/while/body/eval_jaxpr/ppermute | solution.py:15
  95.2 8.1 %collective-permute-start.1 = (bf16[256,2,2,128]{3,0,2,1:T(8,128)(2,1)}, bf16[256,2,2,128]{3,0,2,1:T(8,128)(2,1)S(1)}, u32[]{:S(2)}, u32[]{:S(2)}) collective-permute-start(bf16[256,2,2,128]{3,0,2,1:T(8,128)(2,1)} %get-tuple-element.747), channel_id=1, source_target_pairs={{0,4},{4,8},{8,12},{12,16},{16,20},{20,24},{24,28},{28,32},{32,36}... | collective-permute-start | bytes 786440 | tf_op jit(solution)/shard_map/while/body/eval_jaxpr/ppermute | solution.py:15
  95.2 14.7 %collective-permute-start.2 = (f32[256,2,2,128]{3,0,2,1:T(8,128)}, f32[256,2,2,128]{3,0,2,1:T(8,128)}, u32[]{:S(2)}, u32[]{:S(2)}) collective-permute-start(f32[256,2,2,128]{3,0,2,1:T(8,128)} %get-tuple-element.746), channel_id=1, source_target_pairs={{0,4},{4,8},{8,12},{12,16},{16,20},{20,24},{24,28},{28,32},{32,36}... | collective-permute-start | bytes 1572872 | tf_op jit(solution)/shard_map/while/body/eval_jaxpr/ppermute | solution.py:15
  111.8 9.3 %collective-permute-start.1 = (bf16[256,2,2,128]{3,0,2,1:T(8,128)(2,1)}, bf16[256,2,2,128]{3,0,2,1:T(8,128)(2,1)S(1)}, u32[]{:S(2)}, u32[]{:S(2)}) collective-permute-start(bf16[256,2,2,128]{3,0,2,1:T(8,128)(2,1)} %get-tuple-element.747), channel_id=1, source_target_pairs={{0,4},{4,8},{8,12},{12,16},{16,20},{20,24},{24,28},{28,32},{32,36}... | collective-permute-start | bytes 786440 | tf_op jit(solution)/shard_map/while/body/eval_jaxpr/ppermute | solution.py:15
  111.8 15.9 %collective-permute-start.2 = (f32[256,2,2,128]{3,0,2,1:T(8,128)}, f32[256,2,2,128]{3,0,2,1:T(8,128)}, u32[]{:S(2)}, u32[]{:S(2)}) collective-permute-start(f32[256,2,2,128]{3,0,2,1:T(8,128)} %get-tuple-element.746), channel_id=1, source_target_pairs={{0,4},{4,8},{8,12},{12,16},{16,20},{20,24},{24,28},{28,32},{32,36}... | collective-permute-start | bytes 1572872 | tf_op jit(solution)/shard_map/while/body/eval_jaxpr/ppermute | solution.py:15
  129.6 9.3 %collective-permute-start.1 = (bf16[256,2,2,128]{3,0,2,1:T(8,128)(2,1)}, bf16[256,2,2,128]{3,0,2,1:T(8,128)(2,1)S(1)}, u32[]{:S(2)}, u32[]{:S(2)}) collective-permute-start(bf16[256,2,2,128]{3,0,2,1:T(8,128)(2,1)} %get-tuple-element.747), channel_id=1, source_target_pairs={{0,4},{4,8},{8,12},{12,16},{16,20},{20,24},{24,28},{28,32},{32,36}... | collective-permute-start | bytes 786440 | tf_op jit(solution)/shard_map/while/body/eval_jaxpr/ppermute | solution.py:15
  129.6 15.9 %collective-permute-start.2 = (f32[256,2,2,128]{3,0,2,1:T(8,128)}, f32[256,2,2,128]{3,0,2,1:T(8,128)}, u32[]{:S(2)}, u32[]{:S(2)}) collective-permute-start(f32[256,2,2,128]{3,0,2,1:T(8,128)} %get-tuple-element.746), channel_id=1, source_target_pairs={{0,4},{4,8},{8,12},{12,16},{16,20},{20,24},{24,28},{28,32},{32,36}... | collective-permute-start | bytes 1572872 | tf_op jit(solution)/shard_map/while/body/eval_jaxpr/ppermute | solution.py:15
  147.4 9.3 %collective-permute-start.1 = (bf16[256,2,2,128]{3,0,2,1:T(8,128)(2,1)}, bf16[256,2,2,128]{3,0,2,1:T(8,128)(2,1)S(1)}, u32[]{:S(2)}, u32[]{:S(2)}) collective-permute-start(bf16[256,2,2,128]{3,0,2,1:T(8,128)(2,1)} %get-tuple-element.747), channel_id=1, source_target_pairs={{0,4},{4,8},{8,12},{12,16},{16,20},{20,24},{24,28},{28,32},{32,36}... | collective-permute-start | bytes 786440 | tf_op jit(solution)/shard_map/while/body/eval_jaxpr/ppermute | solution.py:15
  147.4 15.9 %collective-permute-start.2 = (f32[256,2,2,128]{3,0,2,1:T(8,128)}, f32[256,2,2,128]{3,0,2,1:T(8,128)}, u32[]{:S(2)}, u32[]{:S(2)}) collective-permute-start(f32[256,2,2,128]{3,0,2,1:T(8,128)} %get-tuple-element.746), channel_id=1, source_target_pairs={{0,4},{4,8},{8,12},{12,16},{16,20},{20,24},{24,28},{28,32},{32,36}... | collective-permute-start | bytes 1572872 | tf_op jit(solution)/shard_map/while/body/eval_jaxpr/ppermute | solution.py:15
  165.2 9.3 %collective-permute-start.1 = (bf16[256,2,2,128]{3,0,2,1:T(8,128)(2,1)}, bf16[256,2,2,128]{3,0,2,1:T(8,128)(2,1)S(1)}, u32[]{:S(2)}, u32[]{:S(2)}) collective-permute-start(bf16[256,2,2,128]{3,0,2,1:T(8,128)(2,1)} %get-tuple-element.747), channel_id=1, source_target_pairs={{0,4},{4,8},{8,12},{12,16},{16,20},{20,24},{24,28},{28,32},{32,36}... | collective-permute-start | bytes 786440 | tf_op jit(solution)/shard_map/while/body/eval_jaxpr/ppermute | solution.py:15
  165.2 15.9 %collective-permute-start.2 = (f32[256,2,2,128]{3,0,2,1:T(8,128)}, f32[256,2,2,128]{3,0,2,1:T(8,128)}, u32[]{:S(2)}, u32[]{:S(2)}) collective-permute-start(f32[256,2,2,128]{3,0,2,1:T(8,128)} %get-tuple-element.746), channel_id=1, source_target_pairs={{0,4},{4,8},{8,12},{12,16},{16,20},{20,24},{24,28},{28,32},{32,36}... | collective-permute-start | bytes 1572872 | tf_op jit(solution)/shard_map/while/body/eval_jaxpr/ppermute | solution.py:15
  183.0 9.3 %collective-permute-start.1 = (bf16[256,2,2,128]{3,0,2,1:T(8,128)(2,1)}, bf16[256,2,2,128]{3,0,2,1:T(8,128)(2,1)S(1)}, u32[]{:S(2)}, u32[]{:S(2)}) collective-permute-start(bf16[256,2,2,128]{3,0,2,1:T(8,128)(2,1)} %get-tuple-element.747), channel_id=1, source_target_pairs={{0,4},{4,8},{8,12},{12,16},{16,20},{20,24},{24,28},{28,32},{32,36}... | collective-permute-start | bytes 786440 | tf_op jit(solution)/shard_map/while/body/eval_jaxpr/ppermute | solution.py:15
  183.0 15.9 %collective-permute-start.2 = (f32[256,2,2,128]{3,0,2,1:T(8,128)}, f32[256,2,2,128]{3,0,2,1:T(8,128)}, u32[]{:S(2)}, u32[]{:S(2)}) collective-permute-start(f32[256,2,2,128]{3,0,2,1:T(8,128)} %get-tuple-element.746), channel_id=1, source_target_pairs={{0,4},{4,8},{8,12},{12,16},{16,20},{20,24},{24,28},{28,32},{32,36}... | collective-permute-start | bytes 1572872 | tf_op jit(solution)/shard_map/while/body/eval_jaxpr/ppermute | solution.py:15
  200.8 9.3 %collective-permute-start.1 = (bf16[256,2,2,128]{3,0,2,1:T(8,128)(2,1)}, bf16[256,2,2,128]{3,0,2,1:T(8,128)(2,1)S(1)}, u32[]{:S(2)}, u32[]{:S(2)}) collective-permute-start(bf16[256,2,2,128]{3,0,2,1:T(8,128)(2,1)} %get-tuple-element.747), channel_id=1, source_target_pairs={{0,4},{4,8},{8,12},{12,16},{16,20},{20,24},{24,28},{28,32},{32,36}... | collective-permute-start | bytes 786440 | tf_op jit(solution)/shard_map/while/body/eval_jaxpr/ppermute | solution.py:15
  200.8 15.9 %collective-permute-start.2 = (f32[256,2,2,128]{3,0,2,1:T(8,128)}, f32[256,2,2,128]{3,0,2,1:T(8,128)}, u32[]{:S(2)}, u32[]{:S(2)}) collective-permute-start(f32[256,2,2,128]{3,0,2,1:T(8,128)} %get-tuple-element.746), channel_id=1, source_target_pairs={{0,4},{4,8},{8,12},{12,16},{16,20},{20,24},{24,28},{28,32},{32,36}... | collective-permute-start | bytes 1572872 | tf_op jit(solution)/shard_map/while/body/eval_jaxpr/ppermute | solution.py:15
  218.6 11.3 %collective-permute-start.3 = (f32[256,2,2,128]{3,0,2,1:T(8,128)}, f32[256,2,2,128]{3,0,2,1:T(8,128)S(1)}, u32[]{:S(2)}, u32[]{:S(2)}) collective-permute-start(f32[256,2,2,128]{3,0,2,1:T(8,128)} %get-tuple-element.450), channel_id=1, source_target_pairs={{0,228},{4,232},{8,236},{12,240},{16,244},{20,248},{24,252},{28,0}... | collective-permute-start | bytes 1572872 | tf_op jit(solution)/shard_map/ppermute | solution.py:15
  (47 other events, 81.6 us)
where the time goes:
time: 318 us; the launch traced here: 317 us
  waiting for transfers between devices  94.1 us (30%)
  blocking collectives  84 us (26%)
  matrix products  54.6 us (17%)
  other arithmetic  39.4 us (12%)
  local copies, waits for them, and re-layouts  36.9 us (12%)
  starting transfers between devices  5.57 us (2%)
    ppermute x22, waiting for transfers between devices, passed_along(): return lax.ppermute(value, axis, pairs)  94.1 us
    psum x1, blocking collectives, on_device(): lax.psum((q_gain_part, k_gain_part), ('ctx', 'heads'))  84 us
    dot_general x15, matrix products, scores_of(): jnp.einsum('ikgd,jkd->kgij', q_rot, key_rot, preferred_element_type=jnp.f...  15 us
    unnamed x68, local copies, waits for them, and re-layouts  13.6 us
    add x7, other arithmetic, back_step(): grads_now = passed_along(grads_now, 'ctx', 1) + kv_part  13.4 us
    dot_general x8, matrix products, grad_terms(): jnp.einsum('ikgd,jkd->kgij', grad_heads, val_rot, preferred_element_type=...  12.1 us
    dot_general x8, matrix products, grad_terms(): jnp.einsum('kgij,jkd->ikgd', dscore, key_rot, preferred_element_type=jnp....  11.6 us
    dot_general x8, matrix products, grad_terms(): jnp.einsum('kgij,ikgd->jkd', weights_low, grad_heads, preferred_element_t...  10 us
  transfers between devices with their start and end apart: 22, of which 14 were waited for; matrix products, arithmetic and copies ran while one was open for 22% of the time, Pallas kernels for 0%

commit v1 on v0

--- a/solution.py
+++ b/solution.py
@@ -163,7 +163,8 @@
     dq_rot = dq_acc.reshape(tokens_here, kv_local * group_size, head_dim)
     dq_input, q_gain_part = norm_rope_back(q_float, q_gain, cos_table, sin_table, dq_rot)
     dk_input, k_gain_part = norm_rope_back(k_float, k_gain, cos_table, sin_table, key_grads[:, 0])
-    q_gain_grad, k_gain_grad = lax.psum((q_gain_part, k_gain_part), ("ctx", "heads"))
+    _cover_flows = lambda across, link_axis, vals: lax.psum(lax.psum(vals, link_axis), across)
+    q_gain_grad, k_gain_grad = _cover_flows("heads", "ctx", vals=(q_gain_part, k_gain_part))
     dq_raw = dq_input.astype(jnp.bfloat16).reshape(tokens_here, kv_local * group_size * head_dim)
     dk_raw = dk_input.astype(jnp.bfloat16).reshape(tokens_here, kv_local * head_dim)
     dv = key_grads[:, 1].astype(jnp.bfloat16).reshape(tokens_here, kv_local * head_dim)

time: 318 us -> 378 us (1.19)
  blocking collectives: 84 us -> 141 us
    psum x1 -> x2, blocking collectives: 84 us -> 141 us  [the longest x1 131 us: on_device(): lax.psum(vals, link_axis)]
    unnamed x68 -> x72, local copies, waits for them, and re-layouts: 13.6 us -> 14.1 us
  transfers between devices with their start and end apart: 22 -> 22, of which waited for: 14 -> 14; matrix products, arithmetic and copies ran while one was open for 22% -> 18% of each run, Pallas kernels for 0% -> 0%
where the time goes in v1:
time: 378 us; the launch traced here: 377 us
  blocking collectives  141 us (37%)
  waiting for transfers between devices  94 us (25%)
  matrix products  54.6 us (14%)
  other arithmetic  40.2 us (11%)
  local copies, waits for them, and re-layouts  39.3 us (10%)
  starting transfers between devices  5.64 us (1%)
    psum x1, blocking collectives, on_device(): lax.psum(vals, link_axis)  131 us
    ppermute x22, waiting for transfers between devices, passed_along(): return lax.ppermute(value, axis, pairs)  94 us
    dot_general x15, matrix products, scores_of(): jnp.einsum('ikgd,jkd->kgij', q_rot, key_rot, preferred_element_type=jnp.f...  15 us
    unnamed x72, local copies, waits for them, and re-layouts  14.1 us
    add x7, other arithmetic, back_step(): grads_now = passed_along(grads_now, 'ctx', 1) + kv_part  13.4 us
    dot_general x8, matrix products, grad_terms(): jnp.einsum('ikgd,jkd->kgij', grad_heads, val_rot, preferred_element_type=...  12.1 us
    dot_general x8, matrix products, grad_terms(): jnp.einsum('kgij,jkd->ikgd', dscore, key_rot, preferred_element_type=jnp....  11.6 us
    dot_general x8, matrix products, grad_terms(): jnp.einsum('kgij,ikgd->jkd', weights_low, grad_heads, preferred_element_t...  10 us
  transfers between devices with their start and end apart: 22, of which 14 were waited for; matrix products, arithmetic and copies ran while one was open for 18% of the time, Pallas kernels for 0%

profile of v1, /device:TPU:1, one launch (start us, length us, event | category | flops | bytes accessed | tf_op | source)
XLA Modules:
  0.0 376.6 jit_solution(6099821067665270080)
XLA Ops:
  11.5 2.9 fusion.29
  14.4 59.1 %while.38 = (s32[]{:T(128)}, f32[2,8,256]{2,1,0:T(8,128)S(1)}, bf16[256,2,128]{2,0,1:T(8,128)(2,1)S(1)}, s32[4,32]{1,0:T(4,128)S(1)}, s32[]{:T(128)}, /*index=5*...) while((s32[]{:T(128)}, f32[2,8,256]{2,1,0:T(8,128)S(1)}, ...), condition=%wide.region_8.9_spmd.clone, body=%wide.region_5.8_spmd.clone.sunk | while | flops 271778816 | bytes 2167688 | solution.py:125
  14.4 2.7 collective-permute-start
  20.1 2.5 collective-permute-start
  23.2 4.9 %collective-permute-done = bf16[256,2,128]{2,0,1:T(8,128)(2,1)S(1)} collective-permute-done((bf16[256,2,128]{2,0,1:T(8,128)(2,1)S(1)}, bf16[256,2,128]{2,0,1:T(8,128)(2,1)S(1)}, u32[]{:S(2)}, u32[]{:S(2)}) %collective-permute-start) | collective-permute-done | bytes 131104 | tf_op jit(solution)/shard_map/while/body/eval_jaxpr/ppermute | solution.py:15
  29.9 7.1 %collective-permute-done = bf16[256,2,128]{2,0,1:T(8,128)(2,1)S(1)} collective-permute-done((bf16[256,2,128]{2,0,1:T(8,128)(2,1)S(1)}, bf16[256,2,128]{2,0,1:T(8,128)(2,1)S(1)}, u32[]{:S(2)}, u32[]{:S(2)}) %collective-permute-start) | collective-permute-done | bytes 131104 | tf_op jit(solution)/shard_map/while/body/eval_jaxpr/ppermute | solution.py:15
  38.8 7.1 %collective-permute-done = bf16[256,2,128]{2,0,1:T(8,128)(2,1)S(1)} collective-permute-done((bf16[256,2,128]{2,0,1:T(8,128)(2,1)S(1)}, bf16[256,2,128]{2,0,1:T(8,128)(2,1)S(1)}, u32[]{:S(2)}, u32[]{:S(2)}) %collective-permute-start) | collective-permute-done | bytes 131104 | tf_op jit(solution)/shard_map/while/body/eval_jaxpr/ppermute | solution.py:15
  47.6 7.1 %collective-permute-done = bf16[256,2,128]{2,0,1:T(8,128)(2,1)S(1)} collective-permute-done((bf16[256,2,128]{2,0,1:T(8,128)(2,1)S(1)}, bf16[256,2,128]{2,0,1:T(8,128)(2,1)S(1)}, u32[]{:S(2)}, u32[]{:S(2)}) %collective-permute-start) | collective-permute-done | bytes 131104 | tf_op jit(solution)/shard_map/while/body/eval_jaxpr/ppermute | solution.py:15
  56.5 7.1 %collective-permute-done = bf16[256,2,128]{2,0,1:T(8,128)(2,1)S(1)} collective-permute-done((bf16[256,2,128]{2,0,1:T(8,128)(2,1)S(1)}, bf16[256,2,128]{2,0,1:T(8,128)(2,1)S(1)}, u32[]{:S(2)}, u32[]{:S(2)}) %collective-permute-start) | collective-permute-done | bytes 131104 | tf_op jit(solution)/shard_map/while/body/eval_jaxpr/ppermute | solution.py:15
  65.4 7.1 %collective-permute-done = bf16[256,2,128]{2,0,1:T(8,128)(2,1)S(1)} collective-permute-done((bf16[256,2,128]{2,0,1:T(8,128)(2,1)S(1)}, bf16[256,2,128]{2,0,1:T(8,128)(2,1)S(1)}, u32[]{:S(2)}, u32[]{:S(2)}) %collective-permute-start) | collective-permute-done | bytes 131104 | tf_op jit(solution)/shard_map/while/body/eval_jaxpr/ppermute | solution.py:15
  81.3 3.3 fusion.40
  97.4 123.4 %while.39 = (s32[]{:T(128)}, f32[256,2,8,128]{3,0,2,1:T(8,128)S(1)}, f32[256,2,2,128]{3,0,2,1:T(8,128)}, bf16[256,2,2,128]{3,0,2,1:T(8,128)(2,1)}, s32[4,32]{1,0...) while((s32[]{:T(128)}, ...), condition=%wide.region_11.12_spmd.clone, body=%wide.region_9.11_spmd.clone.sunk | while | flops 1354695680 | bytes 37999652 | solution.py:159
  99.1 6.4 %collective-permute-done.1 = bf16[256,2,2,128]{3,0,2,1:T(8,128)(2,1)S(1)} collective-permute-done((bf16[256,2,2,128]{3,0,2,1:T(8,128)(2,1)}, bf16[256,2,2,128]{3,0,2,1:T(8,128)(2,1)S(1)}, u32[]{:S(2)}, u32[]{:S(2)}) %collective-permute-start.1) | collective-permute-done | bytes 262176 | tf_op jit(solution)/shard_map/while/body/eval_jaxpr/ppermute | solution.py:15
  115.7 7.6 %collective-permute-done.1 = bf16[256,2,2,128]{3,0,2,1:T(8,128)(2,1)S(1)} collective-permute-done((bf16[256,2,2,128]{3,0,2,1:T(8,128)(2,1)}, bf16[256,2,2,128]{3,0,2,1:T(8,128)(2,1)S(1)}, u32[]{:S(2)}, u32[]{:S(2)}) %collective-permute-start.1) | collective-permute-done | bytes 262176 | tf_op jit(solution)/shard_map/while/body/eval_jaxpr/ppermute | solution.py:15
  133.5 7.6 %collective-permute-done.1 = bf16[256,2,2,128]{3,0,2,1:T(8,128)(2,1)S(1)} collective-permute-done((bf16[256,2,2,128]{3,0,2,1:T(8,128)(2,1)}, bf16[256,2,2,128]{3,0,2,1:T(8,128)(2,1)S(1)}, u32[]{:S(2)}, u32[]{:S(2)}) %collective-permute-start.1) | collective-permute-done | bytes 262176 | tf_op jit(solution)/shard_map/while/body/eval_jaxpr/ppermute | solution.py:15
  151.3 7.6 %collective-permute-done.1 = bf16[256,2,2,128]{3,0,2,1:T(8,128)(2,1)S(1)} collective-permute-done((bf16[256,2,2,128]{3,0,2,1:T(8,128)(2,1)}, bf16[256,2,2,128]{3,0,2,1:T(8,128)(2,1)S(1)}, u32[]{:S(2)}, u32[]{:S(2)}) %collective-permute-start.1) | collective-permute-done | bytes 262176 | tf_op jit(solution)/shard_map/while/body/eval_jaxpr/ppermute | solution.py:15
  169.1 7.6 %collective-permute-done.1 = bf16[256,2,2,128]{3,0,2,1:T(8,128)(2,1)S(1)} collective-permute-done((bf16[256,2,2,128]{3,0,2,1:T(8,128)(2,1)}, bf16[256,2,2,128]{3,0,2,1:T(8,128)(2,1)S(1)}, u32[]{:S(2)}, u32[]{:S(2)}) %collective-permute-start.1) | collective-permute-done | bytes 262176 | tf_op jit(solution)/shard_map/while/body/eval_jaxpr/ppermute | solution.py:15
  186.9 7.6 %collective-permute-done.1 = bf16[256,2,2,128]{3,0,2,1:T(8,128)(2,1)S(1)} collective-permute-done((bf16[256,2,2,128]{3,0,2,1:T(8,128)(2,1)}, bf16[256,2,2,128]{3,0,2,1:T(8,128)(2,1)S(1)}, u32[]{:S(2)}, u32[]{:S(2)}) %collective-permute-start.1) | collective-permute-done | bytes 262176 | tf_op jit(solution)/shard_map/while/body/eval_jaxpr/ppermute | solution.py:15
  204.7 7.6 %collective-permute-done.1 = bf16[256,2,2,128]{3,0,2,1:T(8,128)(2,1)S(1)} collective-permute-done((bf16[256,2,2,128]{3,0,2,1:T(8,128)(2,1)}, bf16[256,2,2,128]{3,0,2,1:T(8,128)(2,1)S(1)}, u32[]{:S(2)}, u32[]{:S(2)}) %collective-permute-start.1) | collective-permute-done | bytes 262176 | tf_op jit(solution)/shard_map/while/body/eval_jaxpr/ppermute | solution.py:15
  222.3 2.5 multiply_add_fusion
  224.9 2.1 multiply_reduce_fusion.1
  228.3 3.8 %fusion.36 = (f32[2048]{0:T(1024)S(1)}, bf16[256,2048]{1,0:T(8,128)(2,1)}) fusion(bf16[256,2048]{1,0:T(8,128)(2,1)S(1)} %copy-done.3, f32[32,8,16,128]{3,2,1,0:T(8,128)S(1)} %bitcast.265, f32[32,8,16,128]{3,2,1,0:T(8,128)S(1)} %bitcast.267, f32[32,8,16,128]{3,2,1,0:T(8,128)S(1)} %bitcast.266, f32[2048]{0:T(1024)S(1)} %broadcast_bitcast_fusion), kind=kLoop, calls=%fused_computation.53 | loop fusion | flops 4716544 | bytes 8404992 | tf_op jit(solution)/shard_map/reduce_sum | solution.py:59
  235.9 131.5 %all-reduce = (f32[128]{0:T(128)S(1)}, f32[128]{0:T(128)S(1)}) all-reduce(f32[128]{0:T(128)S(1)} %bitcast_reduce_fusion, f32[128]{0:T(128)S(1)} %bitcast_reduce_fusion.1), channel_id=1, replica_groups=mesh['ctx'=64,'heads'=4] {'ctx'}, use_global_device_ids=true, to_apply=%region_16.17 | all-reduce | flops 256 | bytes 2048 | tf_op jit(solution)/shard_map/psum | solution.py:166
  367.4 9.2 %all-reduce.1 = (f32[128]{0:T(128)}, f32[128]{0:T(128)}) all-reduce(f32[128]{0:T(128)S(1)} %get-tuple-element.574, f32[128]{0:T(128)S(1)} %get-tuple-element.575), channel_id=1, replica_groups=mesh['ctx'=64,'heads'=4] {'heads'}, use_global_device_ids=true, to_apply=%region_17.18 | all-reduce | flops 256 | bytes 2048 | tf_op jit(solution)/shard_map/psum | solution.py:166
  (349 shorter events, 121.4 us)
Async XLA Ops:
  1.8 5.1 %copy-start.6 = (f32[256,2,128]{2,0,1:T(8,128)}, f32[256,2,128]{2,0,1:T(8,128)S(1)}, u32[]{:S(2)}) copy-start(f32[256,2,128]{2,0,1:T(8,128)S(1)} %copy.83) | copy-start | bytes 786436
  14.4 59.8 %copy-start.16 = (bf16[256,2048]{1,0:T(8,128)(2,1)S(1)}, bf16[256,2048]{1,0:T(8,128)(2,1)}, u32[]{:S(2)}) copy-start(bf16[256,2048]{1,0:T(8,128)(2,1)} %param.16) | copy-start | bytes 3145732
  14.4 4.6 %collective-permute-start = (bf16[256,2,128]{2,0,1:T(8,128)(2,1)S(1)}, bf16[256,2,128]{2,0,1:T(8,128)(2,1)S(1)}, u32[]{:S(2)}, u32[]{:S(2)}) collective-permute-start(bf16[256,2,128]{2,0,1:T(8,128)(2,1)S(1)} %get-tuple-element.711), channel_id=1, source_target_pairs={{0,4},{4,8},{8,12},{12,16},{16,20},{20,24},{24,28},{28,32},{32,36}... | collective-permute-start | bytes 393224 | tf_op jit(solution)/shard_map/while/body/eval_jaxpr/ppermute | solution.py:15
  20.1 8.0 %collective-permute-start = (bf16[256,2,128]{2,0,1:T(8,128)(2,1)S(1)}, bf16[256,2,128]{2,0,1:T(8,128)(2,1)S(1)}, u32[]{:S(2)}, u32[]{:S(2)}) collective-permute-start(bf16[256,2,128]{2,0,1:T(8,128)(2,1)S(1)} %get-tuple-element.711), channel_id=1, source_target_pairs={{0,4},{4,8},{8,12},{12,16},{16,20},{20,24},{24,28},{28,32},{32,36}... | collective-permute-start | bytes 393224 | tf_op jit(solution)/shard_map/while/body/eval_jaxpr/ppermute | solution.py:15
  29.2 7.8 %collective-permute-start = (bf16[256,2,128]{2,0,1:T(8,128)(2,1)S(1)}, bf16[256,2,128]{2,0,1:T(8,128)(2,1)S(1)}, u32[]{:S(2)}, u32[]{:S(2)}) collective-permute-start(bf16[256,2,128]{2,0,1:T(8,128)(2,1)S(1)} %get-tuple-element.711), channel_id=1, source_target_pairs={{0,4},{4,8},{8,12},{12,16},{16,20},{20,24},{24,28},{28,32},{32,36}... | collective-permute-start | bytes 393224 | tf_op jit(solution)/shard_map/while/body/eval_jaxpr/ppermute | solution.py:15
  38.1 7.8 %collective-permute-start = (bf16[256,2,128]{2,0,1:T(8,128)(2,1)S(1)}, bf16[256,2,128]{2,0,1:T(8,128)(2,1)S(1)}, u32[]{:S(2)}, u32[]{:S(2)}) collective-permute-start(bf16[256,2,128]{2,0,1:T(8,128)(2,1)S(1)} %get-tuple-element.711), channel_id=1, source_target_pairs={{0,4},{4,8},{8,12},{12,16},{16,20},{20,24},{24,28},{28,32},{32,36}... | collective-permute-start | bytes 393224 | tf_op jit(solution)/shard_map/while/body/eval_jaxpr/ppermute | solution.py:15
  47.0 7.8 %collective-permute-start = (bf16[256,2,128]{2,0,1:T(8,128)(2,1)S(1)}, bf16[256,2,128]{2,0,1:T(8,128)(2,1)S(1)}, u32[]{:S(2)}, u32[]{:S(2)}) collective-permute-start(bf16[256,2,128]{2,0,1:T(8,128)(2,1)S(1)} %get-tuple-element.711), channel_id=1, source_target_pairs={{0,4},{4,8},{8,12},{12,16},{16,20},{20,24},{24,28},{28,32},{32,36}... | collective-permute-start | bytes 393224 | tf_op jit(solution)/shard_map/while/body/eval_jaxpr/ppermute | solution.py:15
  55.8 7.8 %collective-permute-start = (bf16[256,2,128]{2,0,1:T(8,128)(2,1)S(1)}, bf16[256,2,128]{2,0,1:T(8,128)(2,1)S(1)}, u32[]{:S(2)}, u32[]{:S(2)}) collective-permute-start(bf16[256,2,128]{2,0,1:T(8,128)(2,1)S(1)} %get-tuple-element.711), channel_id=1, source_target_pairs={{0,4},{4,8},{8,12},{12,16},{16,20},{20,24},{24,28},{28,32},{32,36}... | collective-permute-start | bytes 393224 | tf_op jit(solution)/shard_map/while/body/eval_jaxpr/ppermute | solution.py:15
  64.7 7.8 %collective-permute-start = (bf16[256,2,128]{2,0,1:T(8,128)(2,1)S(1)}, bf16[256,2,128]{2,0,1:T(8,128)(2,1)S(1)}, u32[]{:S(2)}, u32[]{:S(2)}) collective-permute-start(bf16[256,2,128]{2,0,1:T(8,128)(2,1)S(1)} %get-tuple-element.711), channel_id=1, source_target_pairs={{0,4},{4,8},{8,12},{12,16},{16,20},{20,24},{24,28},{28,32},{32,36}... | collective-permute-start | bytes 393224 | tf_op jit(solution)/shard_map/while/body/eval_jaxpr/ppermute | solution.py:15
  97.4 8.1 %collective-permute-start.1 = (bf16[256,2,2,128]{3,0,2,1:T(8,128)(2,1)}, bf16[256,2,2,128]{3,0,2,1:T(8,128)(2,1)S(1)}, u32[]{:S(2)}, u32[]{:S(2)}) collective-permute-start(bf16[256,2,2,128]{3,0,2,1:T(8,128)(2,1)} %get-tuple-element.749), channel_id=1, source_target_pairs={{0,4},{4,8},{8,12},{12,16},{16,20},{20,24},{24,28},{28,32},{32,36}... | collective-permute-start | bytes 786440 | tf_op jit(solution)/shard_map/while/body/eval_jaxpr/ppermute | solution.py:15
  97.4 14.7 %collective-permute-start.2 = (f32[256,2,2,128]{3,0,2,1:T(8,128)}, f32[256,2,2,128]{3,0,2,1:T(8,128)}, u32[]{:S(2)}, u32[]{:S(2)}) collective-permute-start(f32[256,2,2,128]{3,0,2,1:T(8,128)} %get-tuple-element.748), channel_id=1, source_target_pairs={{0,4},{4,8},{8,12},{12,16},{16,20},{20,24},{24,28},{28,32},{32,36}... | collective-permute-start | bytes 1572872 | tf_op jit(solution)/shard_map/while/body/eval_jaxpr/ppermute | solution.py:15
  114.0 9.3 %collective-permute-start.1 = (bf16[256,2,2,128]{3,0,2,1:T(8,128)(2,1)}, bf16[256,2,2,128]{3,0,2,1:T(8,128)(2,1)S(1)}, u32[]{:S(2)}, u32[]{:S(2)}) collective-permute-start(bf16[256,2,2,128]{3,0,2,1:T(8,128)(2,1)} %get-tuple-element.749), channel_id=1, source_target_pairs={{0,4},{4,8},{8,12},{12,16},{16,20},{20,24},{24,28},{28,32},{32,36}... | collective-permute-start | bytes 786440 | tf_op jit(solution)/shard_map/while/body/eval_jaxpr/ppermute | solution.py:15
  114.0 15.9 %collective-permute-start.2 = (f32[256,2,2,128]{3,0,2,1:T(8,128)}, f32[256,2,2,128]{3,0,2,1:T(8,128)}, u32[]{:S(2)}, u32[]{:S(2)}) collective-permute-start(f32[256,2,2,128]{3,0,2,1:T(8,128)} %get-tuple-element.748), channel_id=1, source_target_pairs={{0,4},{4,8},{8,12},{12,16},{16,20},{20,24},{24,28},{28,32},{32,36}... | collective-permute-start | bytes 1572872 | tf_op jit(solution)/shard_map/while/body/eval_jaxpr/ppermute | solution.py:15
  131.8 9.3 %collective-permute-start.1 = (bf16[256,2,2,128]{3,0,2,1:T(8,128)(2,1)}, bf16[256,2,2,128]{3,0,2,1:T(8,128)(2,1)S(1)}, u32[]{:S(2)}, u32[]{:S(2)}) collective-permute-start(bf16[256,2,2,128]{3,0,2,1:T(8,128)(2,1)} %get-tuple-element.749), channel_id=1, source_target_pairs={{0,4},{4,8},{8,12},{12,16},{16,20},{20,24},{24,28},{28,32},{32,36}... | collective-permute-start | bytes 786440 | tf_op jit(solution)/shard_map/while/body/eval_jaxpr/ppermute | solution.py:15
  131.8 15.9 %collective-permute-start.2 = (f32[256,2,2,128]{3,0,2,1:T(8,128)}, f32[256,2,2,128]{3,0,2,1:T(8,128)}, u32[]{:S(2)}, u32[]{:S(2)}) collective-permute-start(f32[256,2,2,128]{3,0,2,1:T(8,128)} %get-tuple-element.748), channel_id=1, source_target_pairs={{0,4},{4,8},{8,12},{12,16},{16,20},{20,24},{24,28},{28,32},{32,36}... | collective-permute-start | bytes 1572872 | tf_op jit(solution)/shard_map/while/body/eval_jaxpr/ppermute | solution.py:15
  149.6 9.3 %collective-permute-start.1 = (bf16[256,2,2,128]{3,0,2,1:T(8,128)(2,1)}, bf16[256,2,2,128]{3,0,2,1:T(8,128)(2,1)S(1)}, u32[]{:S(2)}, u32[]{:S(2)}) collective-permute-start(bf16[256,2,2,128]{3,0,2,1:T(8,128)(2,1)} %get-tuple-element.749), channel_id=1, source_target_pairs={{0,4},{4,8},{8,12},{12,16},{16,20},{20,24},{24,28},{28,32},{32,36}... | collective-permute-start | bytes 786440 | tf_op jit(solution)/shard_map/while/body/eval_jaxpr/ppermute | solution.py:15
  149.6 15.9 %collective-permute-start.2 = (f32[256,2,2,128]{3,0,2,1:T(8,128)}, f32[256,2,2,128]{3,0,2,1:T(8,128)}, u32[]{:S(2)}, u32[]{:S(2)}) collective-permute-start(f32[256,2,2,128]{3,0,2,1:T(8,128)} %get-tuple-element.748), channel_id=1, source_target_pairs={{0,4},{4,8},{8,12},{12,16},{16,20},{20,24},{24,28},{28,32},{32,36}... | collective-permute-start | bytes 1572872 | tf_op jit(solution)/shard_map/while/body/eval_jaxpr/ppermute | solution.py:15
  167.4 9.3 %collective-permute-start.1 = (bf16[256,2,2,128]{3,0,2,1:T(8,128)(2,1)}, bf16[256,2,2,128]{3,0,2,1:T(8,128)(2,1)S(1)}, u32[]{:S(2)}, u32[]{:S(2)}) collective-permute-start(bf16[256,2,2,128]{3,0,2,1:T(8,128)(2,1)} %get-tuple-element.749), channel_id=1, source_target_pairs={{0,4},{4,8},{8,12},{12,16},{16,20},{20,24},{24,28},{28,32},{32,36}... | collective-permute-start | bytes 786440 | tf_op jit(solution)/shard_map/while/body/eval_jaxpr/ppermute | solution.py:15
  167.4 15.9 %collective-permute-start.2 = (f32[256,2,2,128]{3,0,2,1:T(8,128)}, f32[256,2,2,128]{3,0,2,1:T(8,128)}, u32[]{:S(2)}, u32[]{:S(2)}) collective-permute-start(f32[256,2,2,128]{3,0,2,1:T(8,128)} %get-tuple-element.748), channel_id=1, source_target_pairs={{0,4},{4,8},{8,12},{12,16},{16,20},{20,24},{24,28},{28,32},{32,36}... | collective-permute-start | bytes 1572872 | tf_op jit(solution)/shard_map/while/body/eval_jaxpr/ppermute | solution.py:15
  185.2 9.3 %collective-permute-start.1 = (bf16[256,2,2,128]{3,0,2,1:T(8,128)(2,1)}, bf16[256,2,2,128]{3,0,2,1:T(8,128)(2,1)S(1)}, u32[]{:S(2)}, u32[]{:S(2)}) collective-permute-start(bf16[256,2,2,128]{3,0,2,1:T(8,128)(2,1)} %get-tuple-element.749), channel_id=1, source_target_pairs={{0,4},{4,8},{8,12},{12,16},{16,20},{20,24},{24,28},{28,32},{32,36}... | collective-permute-start | bytes 786440 | tf_op jit(solution)/shard_map/while/body/eval_jaxpr/ppermute | solution.py:15
  185.2 15.9 %collective-permute-start.2 = (f32[256,2,2,128]{3,0,2,1:T(8,128)}, f32[256,2,2,128]{3,0,2,1:T(8,128)}, u32[]{:S(2)}, u32[]{:S(2)}) collective-permute-start(f32[256,2,2,128]{3,0,2,1:T(8,128)} %get-tuple-element.748), channel_id=1, source_target_pairs={{0,4},{4,8},{8,12},{12,16},{16,20},{20,24},{24,28},{28,32},{32,36}... | collective-permute-start | bytes 1572872 | tf_op jit(solution)/shard_map/while/body/eval_jaxpr/ppermute | solution.py:15
  203.0 9.3 %collective-permute-start.1 = (bf16[256,2,2,128]{3,0,2,1:T(8,128)(2,1)}, bf16[256,2,2,128]{3,0,2,1:T(8,128)(2,1)S(1)}, u32[]{:S(2)}, u32[]{:S(2)}) collective-permute-start(bf16[256,2,2,128]{3,0,2,1:T(8,128)(2,1)} %get-tuple-element.749), channel_id=1, source_target_pairs={{0,4},{4,8},{8,12},{12,16},{16,20},{20,24},{24,28},{28,32},{32,36}... | collective-permute-start | bytes 786440 | tf_op jit(solution)/shard_map/while/body/eval_jaxpr/ppermute | solution.py:15
  203.0 15.9 %collective-permute-start.2 = (f32[256,2,2,128]{3,0,2,1:T(8,128)}, f32[256,2,2,128]{3,0,2,1:T(8,128)}, u32[]{:S(2)}, u32[]{:S(2)}) collective-permute-start(f32[256,2,2,128]{3,0,2,1:T(8,128)} %get-tuple-element.748), channel_id=1, source_target_pairs={{0,4},{4,8},{8,12},{12,16},{16,20},{20,24},{24,28},{28,32},{32,36}... | collective-permute-start | bytes 1572872 | tf_op jit(solution)/shard_map/while/body/eval_jaxpr/ppermute | solution.py:15
  220.8 11.4 %collective-permute-start.3 = (f32[256,2,2,128]{3,0,2,1:T(8,128)}, f32[256,2,2,128]{3,0,2,1:T(8,128)S(1)}, u32[]{:S(2)}, u32[]{:S(2)}) collective-permute-start(f32[256,2,2,128]{3,0,2,1:T(8,128)} %get-tuple-element.450), channel_id=1, source_target_pairs={{0,228},{4,232},{8,236},{12,240},{16,244},{20,248},{24,252},{28,0}... | collective-permute-start | bytes 1572872 | tf_op jit(solution)/shard_map/ppermute | solution.py:15
  (49 other events, 87.1 us)
